TPU v7x, 128 devices: a whole 4x4x4 slice. The times are simulated.
128 devices in a mesh: strip: 32 (over z_hi, x, y), dict: 4 (over z_lo, core).
Axes of the slice: x: 4, y: 4, z: 4 (z_hi: 2, z_lo: 2; z = z_hi * 2 + z_lo), core: 2. Of those that a mesh axis runs over, the one named last changes fastest.
Arguments:
- patterns: bfloat16 [3600, 256, 512], P(None, 'strip', 'dict'), may hold values from -100 to 160
- scan_mask: int32 [256, 512], P('strip', 'dict'), may hold values 0 or 1
- neighbour_mask: int32 [8, 256, 512], P(None, 'strip', 'dict'), may hold values 0 or 1
- dictionary: bfloat16 [2, 512, 3600], P(None, ('strip', 'dict')), may hold values from -160 to 160
Outputs:
- top_scores: float32 [2, 4, 256, 512], P(None, None, 'strip', 'dict')
All inputs are finite; a program needn't handle non-finite values. No bound on the sum of `scan_mask` or of `neighbour_mask` on one device may be relied on, other than what follows from the above.
Results may differ from a plain program's by a relative error of at most 0.00081.
Values may be sent and summed in bfloat16 or wider, within the bound.
A program may use at most 192 MiB of HBM per device.

v0:
```python
import functools

import jax
import jax.numpy as jnp
import numpy as np
from jax import lax
from jax.experimental import pallas as pl
from jax.experimental.pallas import tpu as pltpu
from jax.sharding import PartitionSpec as P

PH = 60
NPIX = PH * PH
TOP = 4
epsilon = 1e-05
nlpar_scale = 2.0

GROUPS = 15
RUN = 240
RUN_PAD = 256
DEPTH = GROUPS * RUN_PAD
PITCH = 160
LEAD = 336
COLS_DEV = 128
ROWS_DEV = 8
TILES = 7
LANES = TILES * 256
HELD = LEAD + LANES
OFFSETS = tuple(PITCH * a + b for a in (-1, 0, 1) for b in (-1, 0, 1))
NT = (((1,), (1,)), ((), ()))
LIMIT = pltpu.CompilerParams(vmem_limit_bytes=62 << 20)


def tables():
    positions = np.arange(PH, dtype=np.float64)
    spread_px = PH / 8.0
    profile = np.exp(-((positions[:, None] - positions[None, :]) ** 2) / (2.0 * spread_px**2))
    k = profile / profile.sum(axis=1, keepdims=True)
    q = np.arange(RUN)
    d, low = (q // 16) * 4 + (q // 4) % 4, q % 4
    src_a, src_b = q // PH, q % PH
    same = low[:, None] == src_a[None, :]
    first = np.where(same, k[d[:, None], src_b[None, :]], 0.0)
    order = np.where(same & (d[:, None] == src_b[None, :]), 1.0, 0.0)
    e = (q // 16) * 4 + low
    d4 = (q // 4) % 4
    second = np.where(d4[:, None] == d4[None, :], k[e[:, None], e[None, :]], 0.0)
    bf = functools.partial(jnp.asarray, dtype=jnp.bfloat16)
    order_t = np.zeros((RUN, RUN_PAD))
    order_t[:, :RUN] = order.T
    return bf(np.concatenate([first, order])), bf(second), bf(np.eye(256)), bf(order_t)


def standardize_kernel(x_ref, k1_ref, k2_ref, eye_ref, m_ref, s_ref, xs, h, c):
    g = pl.program_id(0)
    for j in range(6):
        xs[pl.ds(j * 320, 320), :] = x_ref[pl.ds(j * 40, 40)].astype(jnp.float32).reshape(320, 128)
    h_at = pl.ds(pl.multiple_of(g * 16, 16), 16)
    for n in range(4):
        even = xs[pl.ds(2 * n, RUN, stride=8), :].astype(jnp.bfloat16)
        odd = xs[pl.ds(2 * n + 1, RUN, stride=8), :].astype(jnp.bfloat16)
        pair = jnp.concatenate([even, odd], axis=1)
        out = jnp.dot(k1_ref[...], pair, preferred_element_type=jnp.float32)
        h[n, :, h_at, :] = out[:RUN].astype(jnp.bfloat16).reshape(GROUPS, 16, 256)
        c[n, g] = out[RUN:].reshape(GROUPS, 16, 256)

    @pl.when(g == GROUPS - 1)
    def _():
        for n in range(4):
            def second(dc, carry):
                total, square = carry
                out = jnp.dot(k2_ref[...], h[n, dc], preferred_element_type=jnp.float32)
                corrected = c[n, :, dc] - out.reshape(GROUPS, 16, 256)
                c[n, :, dc] = corrected
                part = corrected.reshape(2 * GROUPS, 8, 256)
                return total + jnp.sum(part, axis=0), square + jnp.sum(part * part, axis=0)

            zero = jnp.zeros((8, 256), jnp.float32)
            total, square = lax.fori_loop(0, GROUPS, second, (zero, zero))
            mean = jnp.sum(total, axis=0, keepdims=True) / NPIX
            var = jnp.sum(square, axis=0, keepdims=True) / NPIX - mean * mean
            mask = jnp.concatenate([m_ref[2 * n : 2 * n + 1, :], m_ref[2 * n + 1 : 2 * n + 2, :]], axis=1)
            scale = mask.astype(jnp.float32) / jnp.sqrt(jnp.maximum(var, 0.0) + epsilon)
            shift = mean * scale

            def third(ge, carry):
                v = (c[n, ge].reshape(RUN, 256) * scale - shift).astype(jnp.bfloat16)
                v = jnp.concatenate([v, jnp.zeros((16, 256), jnp.bfloat16)], axis=0)
                out = lax.dot_general(eye_ref[...], v, NT, preferred_element_type=jnp.float32)
                at = pl.ds(pl.multiple_of(ge * RUN_PAD, RUN_PAD), RUN_PAD)
                s_ref[pl.ds(256 * n, 256), at] = out.astype(jnp.bfloat16)
                return carry

            lax.fori_loop(0, GROUPS, third, 0)


def standardize(patterns, scan_mask, k1, k2, eye):
    whole = lambda *dims: pl.BlockSpec(dims, lambda g: (0,) * len(dims))
    return pl.pallas_call(
        standardize_kernel,
        grid=(GROUPS,),
        in_specs=[
            pl.BlockSpec((RUN, ROWS_DEV, COLS_DEV), lambda g: (g, 0, 0)),
            whole(2 * RUN, RUN),
            whole(RUN, RUN),
            whole(256, 256),
            whole(ROWS_DEV, COLS_DEV),
        ],
        out_specs=whole(ROWS_DEV * COLS_DEV, DEPTH),
        out_shape=jax.ShapeDtypeStruct((ROWS_DEV * COLS_DEV, DEPTH), jnp.bfloat16),
        scratch_shapes=[
            pltpu.VMEM((RUN * 8, 128), jnp.float32),
            pltpu.VMEM((4, GROUPS, RUN, 256), jnp.bfloat16),
            pltpu.VMEM((4, GROUPS, GROUPS, 16, 256), jnp.float32),
        ],
        compiler_params=LIMIT,
        name="standardize",
    )(patterns, k1, k2, eye, scan_mask)


def prepare_kernel(d_ref, order_ref, o_ref):
    x = jnp.concatenate([d_ref[0].astype(jnp.float32), d_ref[1].astype(jnp.float32)], axis=0)
    inv = 1.0 / jnp.sqrt(jnp.sum(x * x, axis=1, keepdims=True) / NPIX + epsilon)
    hi = inv.astype(jnp.bfloat16).astype(jnp.float32)
    mid = (inv - hi).astype(jnp.bfloat16).astype(jnp.float32)
    low = inv - hi - mid
    xb = x.astype(jnp.bfloat16)
    for ge in range(GROUPS):
        run = xb[:, ge * RUN : (ge + 1) * RUN]
        out = jnp.dot(run, order_ref[...], preferred_element_type=jnp.float32)
        if ge == GROUPS - 1:
            lane = lax.broadcasted_iota(jnp.int32, out.shape, 1)
            for i, piece in enumerate((hi, mid, low)):
                out = jnp.where(lane == RUN + i, piece, out)
        o_ref[:, ge * RUN_PAD : (ge + 1) * RUN_PAD] = out.astype(jnp.bfloat16)


def prepare(dictionary, order_t):
    return pl.pallas_call(
        prepare_kernel,
        out_shape=jax.ShapeDtypeStruct((8, DEPTH), jnp.bfloat16),
        name="prepare",
    )(dictionary, order_t)


def row_start(scan_row):
    return LEAD + PITCH * scan_row


def gram_fields(st, f8):
    row_at = lax.broadcasted_iota(jnp.int32, (136, 128), 0)
    lane_at = lax.broadcasted_iota(jnp.int32, (136, 128), 1)
    slots = {}
    for kk in range(9):
        for low in range(min(kk + 1, 8)):
            slots.setdefault(OFFSETS[kk] - OFFSETS[low], []).append((kk, low))
    f8[...] = jnp.zeros_like(f8)

    def tile(t, carry):
        n0 = pl.multiple_of(t * 256, 256)
        rows = st[pl.ds(n0, LEAD + 256), :]
        cols = st[pl.ds(pl.multiple_of(n0 + LEAD, 16), 256), :]
        g = lax.dot_general(rows, cols, NT, preferred_element_type=jnp.float32)
        for half in range(2):
            lanes = g[:, half * 128 : (half + 1) * 128]
            for o, where_to in slots.items():
                first = LEAD + half * 128 - o
                start = min(first // 8 * 8, LEAD + 256 - 136)
                hit = row_at + (start - first) == lane_at
                value = jnp.sum(jnp.where(hit, lanes[start : start + 136], 0.0), axis=0, keepdims=True)
                at = pl.ds(pl.multiple_of(n0 + half * 128, 128), 128)
                for kk, low in where_to:
                    f8[kk, low : low + 1, at] = value
        return carry

    lax.fori_loop(0, TILES, tile, 0)


def usable_rows(nm_ref, u, first_row, first_col, all_rows, all_cols):
    u[...] = jnp.zeros_like(u)
    kk = lax.broadcasted_iota(jnp.int32, (8, 128), 0)
    kk = kk + (kk >= 4).astype(jnp.int32)
    down = (kk >= 3).astype(jnp.int32) + (kk >= 6).astype(jnp.int32) - 1
    right = kk - 3 * (down + 1) - 1
    col = lax.broadcasted_iota(jnp.int32, (8, 128), 1) + first_col + right
    col_ok = (col >= 0) & (col < all_cols)
    for r in range(ROWS_DEV):
        row = down + (first_row + r)
        ok = (row >= 0) & (row < all_rows) & col_ok & (nm_ref[:, r, :] == 1)
        at = PITCH * (r + 1) + 16
        u[:, at : at + 128] = ok.astype(jnp.float32)


def weigh(f8, u, w):
    def turn(x, off):
        return x if off == 0 else pltpu.roll(x, (-off) % LANES, 1)

    n = f8[0, 0:1, :]
    centre = f8[4]
    placed = {4: centre}
    for kk in (0, 1, 2, 3, 5, 6, 7, 8):
        placed[kk] = turn(f8[kk], OFFSETS[kk])
    last = turn(jnp.broadcast_to(n, (8, LANES)), OFFSETS[8])[0:1]
    own = [placed[kk][kk : kk + 1] if kk < 8 else last for kk in range(9)]
    den = jnp.ones((1, LANES), jnp.float32)
    weights = []
    for kk in range(9):
        if kk == 4:
            value = jnp.ones((1, LANES), jnp.float32)
        else:
            dot = centre[kk : kk + 1] if kk < 4 else placed[kk][4:5]
            distance = (n + own[kk] - 2.0 * dot) / NPIX
            slot = kk if kk < 4 else kk - 1
            value = jnp.where(u[slot : slot + 1, :] > 0.5, jnp.exp(-distance / nlpar_scale), 0.0)
            den = den + value
        weights.append(value)
        w[kk : kk + 1, :] = value
    lows = w[0:8, :]
    quad = jnp.zeros((1, LANES), jnp.float32)
    for kk in range(9):
        part = 2.0 * jnp.sum(lows * placed[kk], axis=0, keepdims=True)
        self_term = weights[kk] * own[kk]
        part = part - self_term if kk < 8 else part + self_term
        quad = quad + weights[kk] * part
    square = jnp.maximum(quad, 0.0) / (den * den) / NPIX
    w[9:10, :] = 1.0 / (jnp.sqrt(square + epsilon) * den * NPIX)


def spread(w, wc, we):
    lane = lax.broadcasted_iota(jnp.int32, (16, 128), 1)
    edge = jnp.zeros((16, 128), jnp.float32)
    kinds = lax.broadcasted_iota(jnp.int32, (16, 128), 0)
    left = (kinds == 0) | (kinds == 3) | (kinds == 6)
    right = (kinds == 2) | (kinds == 5) | (kinds == 8)
    for r in range(ROWS_DEV):
        at = PITCH * (r + 1) + 16
        here = w[:, at : at + 128]
        before = w[:, at + 1 : at + 129]
        after = w[:, at - 1 : at + 127]
        wc[r] = jnp.where(left, before, jnp.where(right, after, here))
        R = r + 1
        edge = jnp.where(lane == 2 * R, pltpu.roll(here, 2 * R, 1), edge)
        edge = jnp.where(lane == 2 * R + 1, pltpu.roll(here, 2 * R + 2, 1), edge)
    odd = lane[0:1] % 2 == 1
    for i in range(3):
        we[i : i + 1, :] = jnp.where(odd, edge[3 * i + 2 : 3 * i + 3], edge[3 * i : 3 * i + 1])


def edge_rows(st, et):
    for R in range(10):
        top = row_start(R)
        tile = st[pl.ds(top, 16), :].astype(jnp.float32)
        et[2 * R : 2 * R + 1, :] = tile[15:16]
        tile = st[pl.ds(top + 144, 16), :].astype(jnp.float32)
        et[2 * R + 1 : 2 * R + 2, :] = tile[0:1]
    et[20:32, :] = jnp.zeros((12, DEPTH), jnp.float32)


def products(d_ref, st, et, p):
    def pair(i, carry):
        a = pl.multiple_of(LEAD + 16 + 2 * PITCH * i, 16)
        b = pl.multiple_of(LEAD + 16 + 2 * PITCH * i + PITCH, 16)
        rows = jnp.concatenate([st[pl.ds(a, 128), :], st[pl.ds(b, 128), :]], axis=0)
        out = lax.dot_general(d_ref[...], rows, NT, preferred_element_type=jnp.float32)
        p[2 * i] = out[:, :128]
        p[2 * i + 1] = out[:, 128:]
        return carry

    lax.fori_loop(0, 5, pair, 0)
    edge = et[...].astype(jnp.bfloat16)
    edge = jnp.concatenate([edge, jnp.zeros((96, DEPTH), jnp.bfloat16)], axis=0)
    p[10] = lax.dot_general(d_ref[...], edge, NT, preferred_element_type=jnp.float32)


def entry_norms(d_ref, inv):
    tail = d_ref[:, DEPTH - 128 :].astype(jnp.float32)
    at = RUN - 128
    value = tail[:, at : at + 1] + tail[:, at + 1 : at + 2] + tail[:, at + 2 : at + 3]
    inv[...] = jnp.broadcast_to(value, inv.shape)


def edge_mix(p, we):
    def step(k, carry):
        at = pl.ds(pl.multiple_of(k * 8, 8), 8)
        e = p[10, at, :]
        mix = e * we[1:2, :] + pltpu.roll(e, 2, 1) * we[0:1, :] + pltpu.roll(e, 126, 1) * we[2:3, :]
        p[10, at, :] = mix
        return carry

    lax.fori_loop(0, 128, step, 0, unroll=8)


def best_scores(p, inv, wc, o_ref):
    lane = lax.broadcasted_iota(jnp.int32, (8, 128), 1)
    first, last = lane == 0, lane == 127
    for r in range(ROWS_DEV):
        wt = [jnp.broadcast_to(wc[r, kk : kk + 1, :], (8, 128)) for kk in range(9)]
        R = r + 1

        def step(k, best):
            at = pl.ds(pl.multiple_of(k * 8, 8), 8)
            up, mid, down = p[r, at, :], p[r + 1, at, :], p[r + 2, at, :]
            edge = pltpu.roll(p[10, at, :], 127 - 2 * R, 1)
            left = up * wt[0] + mid * wt[3] + down * wt[6]
            right = up * wt[2] + mid * wt[5] + down * wt[8]
            here = up * wt[1] + mid + down * wt[7]
            left = jnp.where(last, edge, left)
            right = jnp.where(first, edge, right)
            v = (here + pltpu.roll(left, 1, 1) + pltpu.roll(right, 127, 1)) * inv[at, :]
            b0, b1, b2, b3 = best
            n0, v = jnp.maximum(b0, v), jnp.minimum(b0, v)
            n1, v = jnp.maximum(b1, v), jnp.minimum(b1, v)
            n2, v = jnp.maximum(b2, v), jnp.minimum(b2, v)
            return n0, n1, n2, jnp.maximum(b3, v)

        low = jnp.full((8, 128), -jnp.inf, jnp.float32)
        best = lax.fori_loop(0, 128, step, (low, low, low, low), unroll=4)
        for shift in (6, 7):
            other = [pltpu.roll(b, shift, 0) for b in best]
            m = [jnp.maximum(best[i], other[3 - i]) for i in range(4)]
            h0, l0 = jnp.maximum(m[0], m[2]), jnp.minimum(m[0], m[2])
            h1, l1 = jnp.maximum(m[1], m[3]), jnp.minimum(m[1], m[3])
            best = (jnp.maximum(h0, h1), jnp.minimum(h0, h1), jnp.maximum(l0, l1), jnp.minimum(l0, l1))
        scale = wc[r, 9:10, :]
        for j in range(TOP):
            o_ref[0, j, r : r + 1, :] = best[j][0:1] * scale
            o_ref[1, j, r : r + 1, :] = best[j][4:5] * scale


def index_kernel(rows_axis, cols_axis, s_hbm, up_hbm, down_hbm, left_hbm, right_hbm, d_ref, nm_ref, o_ref,
                 st, et, p, f8, u, w, wc, we, inv, sem):
    copies = []
    for r in range(ROWS_DEV):
        copies.append((s_hbm.at[pl.ds(128 * r, 128), :], st.at[pl.ds(row_start(r + 1) + 16, 128), :]))
    copies.append((up_hbm, st.at[pl.ds(row_start(0) + 16, 128), :]))
    copies.append((down_hbm, st.at[pl.ds(row_start(9) + 16, 128), :]))
    for R in range(10):
        copies.append((left_hbm.at[R], st.at[pl.ds(row_start(R), 16), :]))
        copies.append((right_hbm.at[R], st.at[pl.ds(row_start(R) + 144, 16), :]))
    started = [pltpu.make_async_copy(a, b, sem.at[i]) for i, (a, b) in enumerate(copies)]
    for copy in started:
        copy.start()
    st[pl.ds(0, LEAD), :] = jnp.zeros((LEAD, DEPTH), jnp.bfloat16)
    st[pl.ds(LEAD + 10 * PITCH, LANES - 10 * PITCH), :] = jnp.zeros((LANES - 10 * PITCH, DEPTH), jnp.bfloat16)
    first_row = lax.axis_index(rows_axis) * ROWS_DEV
    first_col = lax.axis_index(cols_axis) * COLS_DEV
    usable_rows(nm_ref, u, first_row, first_col, lax.axis_size(rows_axis) * ROWS_DEV, lax.axis_size(cols_axis) * COLS_DEV)
    for copy in started:
        copy.wait()
    w[...] = jnp.zeros_like(w)
    gram_fields(st, f8)
    weigh(f8, u, w)
    spread(w, wc, we)
    edge_rows(st, et)
    products(d_ref, st, et, p)
    entry_norms(d_ref, inv)
    edge_mix(p, we)
    best_scores(p, inv, wc, o_ref)


INDEX_SCRATCH = [
    pltpu.VMEM((HELD, DEPTH), jnp.bfloat16),
    pltpu.VMEM((32, DEPTH), jnp.float32),
    pltpu.VMEM((11, 1024, 128), jnp.float32),
    pltpu.VMEM((9, 8, LANES), jnp.float32),
    pltpu.VMEM((8, LANES), jnp.float32),
    pltpu.VMEM((16, LANES), jnp.float32),
    pltpu.VMEM((8, 16, 128), jnp.float32),
    pltpu.VMEM((8, 128), jnp.float32),
    pltpu.VMEM((1024, 128), jnp.float32),
]


def index_patterns(s, up, down, left, right, d, neighbour_mask):
    anywhere = pl.BlockSpec(memory_space=pl.ANY)
    vmem = pl.BlockSpec(memory_space=pltpu.VMEM)
    return pl.pallas_call(
        functools.partial(index_kernel, "strip", "dict"),
        in_specs=[anywhere] * 5 + [vmem, vmem],
        out_specs=vmem,
        out_shape=jax.ShapeDtypeStruct((2, TOP, ROWS_DEV, COLS_DEV), jnp.float32),
        scratch_shapes=INDEX_SCRATCH + [pltpu.SemaphoreType.DMA((30,))],
        compiler_params=LIMIT,
        name="index",
    )(s, up, down, left, right, d, neighbour_mask)


def gather_entries(mine):
    copies = jnp.broadcast_to(mine, (lax.axis_size("dict"), *mine.shape))
    grouped = lax.all_to_all(copies, "dict", split_axis=0, concat_axis=0, tiled=True)
    return lax.all_gather(grouped.reshape(-1, DEPTH), "strip", axis=0, tiled=True)


def shift(value, axis, step):
    count = lax.axis_size(axis)
    return lax.ppermute(value, axis, [(i, (i + step) % count) for i in range(count)])


def on_device(patterns, scan_mask, neighbour_mask, dictionary):
    k1, k2, eye, order_t = tables()
    d = gather_entries(prepare(dictionary, order_t))
    s = standardize(patterns, scan_mask, k1, k2, eye)
    up = shift(s[-128:], "strip", 1)
    down = shift(s[:128], "strip", -1)
    rows = jnp.concatenate([up[None], s.reshape(8, 128, DEPTH), down[None]], axis=0)
    left = shift(rows[:, 112:], "dict", 1)
    right = shift(rows[:, :16], "dict", -1)
    return index_patterns(s, up, down, left, right, d, neighbour_mask)


def solution(mesh):
    in_specs = (
        P(None, "strip", "dict"),
        P("strip", "dict"),
        P(None, "strip", "dict"),
        P(None, ("strip", "dict"), None),
    )
    out_specs = P(None, None, "strip", "dict")
    return jax.shard_map(
        on_device, mesh=mesh, in_specs=in_specs, out_specs=out_specs, check_vma=False
    )
```

profile of v0, /device:TPU:1, one launch (start us, length us, event | category | flops | bytes accessed | tf_op | source)
XLA Modules:
  0.0 244.7 jit_solution(11484554773321814703)
XLA Ops:
  6.5 0.0 all-gather.2.cloned.1.call-start
  6.5 1.9 prepare.1
  8.5 0.8 broadcast_in_dim.11
  9.3 9.4 %all_to_all.5 = bf16[4,8,3840]{2,1,0:T(8,128)(2,1)} all-to-all(bf16[4,8,3840]{2,1,0:T(8,128)(2,1)S(1)} %broadcast_in_dim.11), channel_id=1, replica_groups=mesh['strip'=32,'dict'=4] {'dict'}, dimensions={0} | all-to-all | bytes 491520 | tf_op jit(solution)/shard_map/all_to_all | solution.py:389
  18.7 0.0 all-gather.2.cloned.1.call-update
  18.8 42.0 %standardize.1.s_hbm = bf16[1024,3840]{1,0:T(8,128)(2,1)} custom-call(bf16[3600,8,128]{2,1,0:T(8,128)(2,1)} %x_ref.1, bf16[480,240]{1,0:T(8,128)(2,1)} %constant.8.clone.k1_ref, bf16[240,240]{1,0:T(8,128)(2,1)} %constant.9.clone.k2_ref, bf16[256,256]{1,0:T(8,128)(2,1)} %constant.10.clone.eye_ref, s32[8,128]{1,0:T(8,128)} %m_ref.1), custom_call_target="tpu_custom_call" | custom-call | tf_op jit(solution)/shard_map/standardize/pallas_call | solution.py:98
  60.7 1.6 fusion
  62.4 1.4 collective-permute-start
  63.7 7.0 %collective-permute-start.1 = (bf16[128,3840]{1,0:T(8,128)(2,1)S(1)}, bf16[128,3840]{1,0:T(8,128)(2,1)S(1)}, u32[]{:S(2)}, u32[]{:S(2)}) collective-permute-start(bf16[128,3840]{1,0:T(8,128)(2,1)S(1)} %get-tuple-element.7), channel_id=1, source_target_pairs={{0,124},{4,0},{8,4},{12,8},{16,12},{20,16},{24,20},{28,24},{32,28}... | collective-permute-start | bytes 2949128 | tf_op jit(solution)/shard_map/ppermute | solution.py:395
  70.7 21.4 %collective-permute-done.up_hbm = bf16[128,3840]{1,0:T(8,128)(2,1)S(1)} collective-permute-done((bf16[128,3840]{1,0:T(8,128)(2,1)S(1)}, bf16[128,3840]{1,0:T(8,128)(2,1)S(1)}, u32[]{:S(2)}, u32[]{:S(2)}) %collective-permute-start) | collective-permute-done | bytes 983072 | tf_op jit(solution)/shard_map/ppermute | solution.py:395
  92.1 0.0 copy-start
  92.1 0.0 collective-permute-done.1.down_hbm
  92.1 0.0 copy-start.1
  92.1 2.4 pad_maximum_fusion
  94.5 0.0 copy-done
  94.5 0.0 copy-done.1
  94.5 2.0 collective-permute-start.2
  96.5 0.0 collective-permute-start.3
  96.5 52.3 %collective-permute-done.2.left_hbm = bf16[10,16,3840]{2,1,0:T(8,128)(2,1)S(1)} collective-permute-done((bf16[10,16,3840]{2,1,0:T(8,128)(2,1)S(1)}, bf16[10,16,3840]{2,1,0:T(8,128)(2,1)S(1)}, u32[]{:S(2)}, u32[]{:S(2)}) %collective-permute-start.2) | collective-permute-done | bytes 1228832 | tf_op jit(solution)/shard_map/ppermute | solution.py:395
  148.8 0.0 copy-start.2
  148.8 2.8 %collective-permute-done.3.right_hbm = bf16[10,16,3840]{2,1,0:T(8,128)(2,1)} collective-permute-done((bf16[10,16,3840]{2,1,0:T(8,128)(2,1)S(1)}, bf16[10,16,3840]{2,1,0:T(8,128)(2,1)}, u32[]{:S(2)}, u32[]{:S(2)}) %collective-permute-start.3) | collective-permute-done | bytes 1228832 | tf_op jit(solution)/shard_map/ppermute | solution.py:395
  151.6 13.2 %all-gather.2.cloned.1.call-done.d_ref = bf16[1024,3840]{1,0:T(8,128)(2,1)} async-done(((bf16[32,3840]{1,0:T(8,128)(2,1)}), bf16[1024,3840]{1,0:T(8,128)(2,1)}) %all-gather.2.cloned.1.call-update) | async-done | bytes 7864336 | tf_op jit(solution)/shard_map/all_gather | solution.py:390
  164.8 0.0 copy-done.2
  164.8 73.0 %index.1 = f32[2,4,8,128]{3,2,1,0:T(8,128)} custom-call(bf16[1024,3840]{1,0:T(8,128)(2,1)} %standardize.1.s_hbm, bf16[128,3840]{1,0:T(8,128)(2,1)} %copy-done, bf16[128,3840]{1,0:T(8,128)(2,1)} %copy-done.1, bf16[10,16,3840]{2,1,0:T(8,128)(2,1)} %copy-done.2, bf16[10,16,3840]{2,1,0:T(8,128)(2,1)} %collective-permute-done.3.right_hbm, ...), custom_call_target="tpu_custom_call" | custom-call | tf_op jit(solution)/shard_map/index/pallas_call | solution.py:376
Async XLA Ops:
  6.5 158.2 %all-gather.2.cloned.1.call-start = ((), (), s32[]{:S(2)}) async-start(), calls=%async_computation.1 | async-start | bytes 8110080 | tf_op jit(solution)/shard_map/all_gather | solution.py:390
  62.4 29.7 %collective-permute-start = (bf16[128,3840]{1,0:T(8,128)(2,1)S(1)}, bf16[128,3840]{1,0:T(8,128)(2,1)S(1)}, u32[]{:S(2)}, u32[]{:S(2)}) collective-permute-start(bf16[128,3840]{1,0:T(8,128)(2,1)S(1)} %get-tuple-element.8), channel_id=1, source_target_pairs={{0,4},{4,8},{8,12},{12,16},{16,20},{20,24},{24,28},{28,32},{32,36}... | collective-permute-start | bytes 2949128 | tf_op jit(solution)/shard_map/ppermute | solution.py:395
  63.7 28.4 %collective-permute-start.1 = (bf16[128,3840]{1,0:T(8,128)(2,1)S(1)}, bf16[128,3840]{1,0:T(8,128)(2,1)S(1)}, u32[]{:S(2)}, u32[]{:S(2)}) collective-permute-start(bf16[128,3840]{1,0:T(8,128)(2,1)S(1)} %get-tuple-element.7), channel_id=1, source_target_pairs={{0,124},{4,0},{8,4},{12,8},{16,12},{20,16},{24,20},{28,24},{32,28}... | collective-permute-start | bytes 2949128 | tf_op jit(solution)/shard_map/ppermute | solution.py:395
  92.1 2.4 copy-start
  92.1 2.4 copy-start.1
  94.5 54.3 %collective-permute-start.2 = (bf16[10,16,3840]{2,1,0:T(8,128)(2,1)S(1)}, bf16[10,16,3840]{2,1,0:T(8,128)(2,1)S(1)}, u32[]{:S(2)}, u32[]{:S(2)}) collective-permute-start(bf16[10,16,3840]{2,1,0:T(8,128)(2,1)S(1)} %get-tuple-element.6), channel_id=1, source_target_pairs={{0,1},{1,2},{2,3},{3,0},{4,5},{5,6},{6,7},{7,4},{8,9},{9,10},{10,1... | collective-permute-start | bytes 3686408 | tf_op jit(solution)/shard_map/ppermute | solution.py:395
  96.5 55.1 %collective-permute-start.3 = (bf16[10,16,3840]{2,1,0:T(8,128)(2,1)S(1)}, bf16[10,16,3840]{2,1,0:T(8,128)(2,1)}, u32[]{:S(2)}, u32[]{:S(2)}) collective-permute-start(bf16[10,16,3840]{2,1,0:T(8,128)(2,1)S(1)} %get-tuple-element.5), channel_id=1, source_target_pairs={{0,3},{1,0},{2,1},{3,2},{4,7},{5,4},{6,5},{7,6},{8,11},{9,8},{10,9... | collective-permute-start | bytes 3686408 | tf_op jit(solution)/shard_map/ppermute | solution.py:395
  148.8 16.0 %copy-start.2 = (bf16[10,16,3840]{2,1,0:T(8,128)(2,1)}, bf16[10,16,3840]{2,1,0:T(8,128)(2,1)S(1)}, u32[]{:S(2)}) copy-start(bf16[10,16,3840]{2,1,0:T(8,128)(2,1)S(1)} %collective-permute-done.2.left_hbm) | copy-start | bytes 3686404
Sparse Core Ops, SparseCore 0:
  18.9 145.8 all-gather.1
where the time goes:
time: 247 us; the launch traced here: 245 us
  Pallas kernels  117 us (47%)
  waiting for transfers between devices  89.6 us (36%)
  between operations  13.4 us (5%)
  starting transfers between devices  10.4 us (4%)
  blocking collectives  9.42 us (4%)
  local copies, waits for them, and re-layouts  2.48 us (1%)
    ppermute x4, waiting for transfers between devices, shift(): lax.ppermute(value, axis, [(i, (i + step) % count) for i in range(count)])  76.5 us
    pallas_call x1, Pallas kernels, index_patterns(): pl.pallas_call(functools.partial(index_kernel, 'strip', 'dict'), in_specs...  73 us
    pallas_call x1, Pallas kernels, standardize(): pl.pallas_call(standardize_kernel, grid=(GROUPS,), in_specs=[pl.BlockSpec...  42 us
    all_gather x1, waiting for transfers between devices, gather_entries(): lax.all_gather(grouped.reshape(-1, DEPTH), 'strip', axis=0, tiled=True)  13.2 us
    ppermute x4, starting transfers between devices, shift(): lax.ppermute(value, axis, [(i, (i + step) % count) for i in range(count)])  10.4 us
    all_to_all x1, blocking collectives, gather_entries(): lax.all_to_all(copies, 'dict', split_axis=0, concat_axis=0, tiled=True)  9.42 us
  transfers between devices with their start and end apart: 5, of which 4 were waited for; matrix products, arithmetic and copies ran while one was open for 2% of the time, Pallas kernels for 17%

commit v1 on v0

v1 whole, which is shorter than its diff:
```python
import functools

import jax
import jax.numpy as jnp
import numpy as np
from jax import lax
from jax.experimental import pallas as pl
from jax.experimental.pallas import tpu as pltpu
from jax.sharding import PartitionSpec as P

PH = 60
NPIX = PH * PH
TOP = 4
epsilon = 1e-05
nlpar_scale = 2.0

GROUPS = 15
RUN = 240
RUN_PAD = 256
DEPTH = GROUPS * RUN_PAD
PITCH = 160
LEAD = 336
COLS_DEV = 128
ROWS_DEV = 8
TILES = 7
LANES = TILES * 256
HELD = LEAD + LANES
OFFSETS = tuple(PITCH * a + b for a in (-1, 0, 1) for b in (-1, 0, 1))
NT = (((1,), (1,)), ((), ()))


def tables():
    positions = np.arange(PH, dtype=np.float64)
    spread_px = PH / 8.0
    profile = np.exp(-((positions[:, None] - positions[None, :]) ** 2) / (2.0 * spread_px**2))
    k = profile / profile.sum(axis=1, keepdims=True)
    q = np.arange(RUN)
    d, low = (q // 16) * 4 + (q // 4) % 4, q % 4
    src_a, src_b = q // PH, q % PH
    same = low[:, None] == src_a[None, :]
    first = np.where(same, k[d[:, None], src_b[None, :]], 0.0)
    order = np.where(same & (d[:, None] == src_b[None, :]), 1.0, 0.0)
    e = (q // 16) * 4 + low
    d4 = (q // 4) % 4
    second = np.where(d4[:, None] == d4[None, :], k[e[:, None], e[None, :]], 0.0)
    bf = functools.partial(jnp.asarray, dtype=jnp.bfloat16)
    order_t = np.zeros((RUN, RUN_PAD))
    order_t[:, :RUN] = order.T
    return bf(np.concatenate([first, order])), bf(second), bf(np.eye(256)), bf(order_t)


def prepare(d_ref, order_ref, own):
    x = jnp.concatenate([d_ref[0].astype(jnp.float32), d_ref[1].astype(jnp.float32)], axis=0)
    inv = 1.0 / jnp.sqrt(jnp.sum(x * x, axis=1, keepdims=True) / NPIX + epsilon)
    hi = inv.astype(jnp.bfloat16).astype(jnp.float32)
    mid = (inv - hi).astype(jnp.bfloat16).astype(jnp.float32)
    low = inv - hi - mid
    xb = x.astype(jnp.bfloat16)
    for ge in range(GROUPS):
        run = xb[:, ge * RUN : (ge + 1) * RUN]
        out = jnp.dot(run, order_ref[...], preferred_element_type=jnp.float32)
        if ge == GROUPS - 1:
            lane = lax.broadcasted_iota(jnp.int32, out.shape, 1)
            for i, piece in enumerate((hi, mid, low)):
                out = jnp.where(lane == RUN + i, piece, out)
        own[:, ge * RUN_PAD : (ge + 1) * RUN_PAD] = out


def first_pass(g, x_ref, k1_ref, xs, h, c):
    for j in range(6):
        xs[pl.ds(j * 320, 320), :] = x_ref[pl.ds(j * 40, 40)].astype(jnp.float32).reshape(320, 128)
    h_at = pl.ds(pl.multiple_of(g * 16, 16), 16)
    for n in range(4):
        even = xs[pl.ds(2 * n, RUN, stride=8), :].astype(jnp.bfloat16)
        odd = xs[pl.ds(2 * n + 1, RUN, stride=8), :].astype(jnp.bfloat16)
        pair = jnp.concatenate([even, odd], axis=1)
        out = jnp.dot(k1_ref[...], pair, preferred_element_type=jnp.float32)
        h[n, :, h_at, :] = out[:RUN].astype(jnp.bfloat16).reshape(GROUPS, 16, 256)
        c[n, g] = out[RUN:].reshape(GROUPS, 16, 256)


def second_pass(n, k2_ref, eye_ref, m_ref, h, c, st):
    def second(dc, carry):
        total, square = carry
        out = jnp.dot(k2_ref[...], h[n, dc], preferred_element_type=jnp.float32)
        corrected = c[n, :, dc] - out.reshape(GROUPS, 16, 256)
        c[n, :, dc] = corrected
        part = corrected.reshape(2 * GROUPS, 8, 256)
        return total + jnp.sum(part, axis=0), square + jnp.sum(part * part, axis=0)

    zero = jnp.zeros((8, 256), jnp.float32)
    total, square = lax.fori_loop(0, GROUPS, second, (zero, zero))
    mean = jnp.sum(total, axis=0, keepdims=True) / NPIX
    var = jnp.sum(square, axis=0, keepdims=True) / NPIX - mean * mean
    mask = jnp.concatenate([m_ref[2 * n : 2 * n + 1, :], m_ref[2 * n + 1 : 2 * n + 2, :]], axis=1)
    scale = mask.astype(jnp.float32) / jnp.sqrt(jnp.maximum(var, 0.0) + epsilon)
    shift = mean * scale

    def third(ge, carry):
        v = (c[n, ge].reshape(RUN, 256) * scale - shift).astype(jnp.bfloat16)
        v = jnp.concatenate([v, jnp.zeros((16, 256), jnp.bfloat16)], axis=0)
        out = lax.dot_general(eye_ref[...], v, NT, preferred_element_type=jnp.float32)
        out = out.astype(jnp.bfloat16)
        at = pl.ds(pl.multiple_of(ge * RUN_PAD, RUN_PAD), RUN_PAD)
        st[pl.ds(own_start(2 * n), 128), at] = out[:128]
        st[pl.ds(own_start(2 * n + 1), 128), at] = out[128:]
        return carry

    lax.fori_loop(0, GROUPS, third, 0)


def row_start(scan_row):
    return LEAD + PITCH * scan_row


def own_start(r):
    return row_start(r + 1) + 16


def gram_fields(st, f8):
    row_at = lax.broadcasted_iota(jnp.int32, (136, 128), 0)
    lane_at = lax.broadcasted_iota(jnp.int32, (136, 128), 1)
    slots = {}
    for kk in range(9):
        for low in range(min(kk + 1, 8)):
            slots.setdefault(OFFSETS[kk] - OFFSETS[low], []).append((kk, low))
    f8[...] = jnp.zeros_like(f8)

    def tile(t, carry):
        n0 = pl.multiple_of(t * 256, 256)
        rows = st[pl.ds(n0, LEAD + 256), :]
        cols = st[pl.ds(pl.multiple_of(n0 + LEAD, 16), 256), :]
        g = lax.dot_general(rows, cols, NT, preferred_element_type=jnp.float32)
        for half in range(2):
            lanes = g[:, half * 128 : (half + 1) * 128]
            for o, where_to in slots.items():
                first = LEAD + half * 128 - o
                start = min(first // 8 * 8, LEAD + 256 - 136)
                hit = row_at + (start - first) == lane_at
                value = jnp.sum(jnp.where(hit, lanes[start : start + 136], 0.0), axis=0, keepdims=True)
                at = pl.ds(pl.multiple_of(n0 + half * 128, 128), 128)
                for kk, low in where_to:
                    f8[kk, low : low + 1, at] = value
        return carry

    lax.fori_loop(0, TILES, tile, 0)


def usable_rows(nm_ref, u, first_row, first_col, all_rows, all_cols):
    u[...] = jnp.zeros_like(u)
    kk = lax.broadcasted_iota(jnp.int32, (8, 128), 0)
    kk = kk + (kk >= 4).astype(jnp.int32)
    down = (kk >= 3).astype(jnp.int32) + (kk >= 6).astype(jnp.int32) - 1
    right = kk - 3 * (down + 1) - 1
    col = lax.broadcasted_iota(jnp.int32, (8, 128), 1) + first_col + right
    col_ok = (col >= 0) & (col < all_cols)
    for r in range(ROWS_DEV):
        row = down + (first_row + r)
        ok = (row >= 0) & (row < all_rows) & col_ok & (nm_ref[:, r, :] == 1)
        at = PITCH * (r + 1) + 16
        u[:, at : at + 128] = ok.astype(jnp.float32)


def weigh(f8, u, w):
    def turn(x, off):
        return x if off == 0 else pltpu.roll(x, (-off) % LANES, 1)

    n = f8[0, 0:1, :]
    centre = f8[4]
    placed = {4: centre}
    for kk in (0, 1, 2, 3, 5, 6, 7, 8):
        placed[kk] = turn(f8[kk], OFFSETS[kk])
    last = turn(jnp.broadcast_to(n, (8, LANES)), OFFSETS[8])[0:1]
    own = [placed[kk][kk : kk + 1] if kk < 8 else last for kk in range(9)]
    den = jnp.ones((1, LANES), jnp.float32)
    weights = []
    for kk in range(9):
        if kk == 4:
            value = jnp.ones((1, LANES), jnp.float32)
        else:
            dot = centre[kk : kk + 1] if kk < 4 else placed[kk][4:5]
            distance = (n + own[kk] - 2.0 * dot) / NPIX
            slot = kk if kk < 4 else kk - 1
            value = jnp.where(u[slot : slot + 1, :] > 0.5, jnp.exp(-distance / nlpar_scale), 0.0)
            den = den + value
        weights.append(value)
        w[kk : kk + 1, :] = value
    lows = w[0:8, :]
    quad = jnp.zeros((1, LANES), jnp.float32)
    for kk in range(9):
        part = 2.0 * jnp.sum(lows * placed[kk], axis=0, keepdims=True)
        self_term = weights[kk] * own[kk]
        part = part - self_term if kk < 8 else part + self_term
        quad = quad + weights[kk] * part
    square = jnp.maximum(quad, 0.0) / (den * den) / NPIX
    w[9:10, :] = 1.0 / (jnp.sqrt(square + epsilon) * den * NPIX)


def spread(w, wc, we):
    lane = lax.broadcasted_iota(jnp.int32, (16, 128), 1)
    edge = jnp.zeros((16, 128), jnp.float32)
    kinds = lax.broadcasted_iota(jnp.int32, (16, 128), 0)
    left = (kinds == 0) | (kinds == 3) | (kinds == 6)
    right = (kinds == 2) | (kinds == 5) | (kinds == 8)
    for r in range(ROWS_DEV):
        at = PITCH * (r + 1) + 16
        here = w[:, at : at + 128]
        before = w[:, at + 1 : at + 129]
        after = w[:, at - 1 : at + 127]
        wc[r] = jnp.where(left, before, jnp.where(right, after, here))
        R = r + 1
        edge = jnp.where(lane == 2 * R, pltpu.roll(here, 2 * R, 1), edge)
        edge = jnp.where(lane == 2 * R + 1, pltpu.roll(here, 2 * R + 2, 1), edge)
    odd = lane[0:1] % 2 == 1
    for i in range(3):
        we[i : i + 1, :] = jnp.where(odd, edge[3 * i + 2 : 3 * i + 3], edge[3 * i : 3 * i + 1])


def own_edges(st, et, eout):
    for r in range(ROWS_DEV):
        top = own_start(r)
        et[r : r + 1, :] = st[pl.ds(top, 16), :].astype(jnp.float32)[0:1]
        et[16 + r : 17 + r, :] = st[pl.ds(top + 112, 16), :].astype(jnp.float32)[15:16]
    et[8:16, :] = jnp.zeros((8, DEPTH), jnp.float32)
    et[24:32, :] = jnp.zeros((8, DEPTH), jnp.float32)
    eout[0] = et[0:16, :].astype(jnp.bfloat16)
    eout[1] = et[16:32, :].astype(jnp.bfloat16)


def place_edges(R, left, right, st, et):
    et[2 * R : 2 * R + 1, :] = left
    et[2 * R + 1 : 2 * R + 2, :] = right
    st[pl.ds(row_start(R), 16), :] = jnp.broadcast_to(left, (16, DEPTH)).astype(jnp.bfloat16)
    st[pl.ds(row_start(R) + 144, 16), :] = jnp.broadcast_to(right, (16, DEPTH)).astype(jnp.bfloat16)


def inner_edges(ein, st, et, cout):
    left, right = ein[0].astype(jnp.float32), ein[1].astype(jnp.float32)
    row = lax.broadcasted_iota(jnp.int32, (16, DEPTH), 0)
    for i, r in enumerate((0, ROWS_DEV - 1)):
        both = jnp.where(row == 0, left[r : r + 1], right[r : r + 1])
        cout[i] = both.astype(jnp.bfloat16)
    for r in range(ROWS_DEV):
        place_edges(r + 1, left[r : r + 1], right[r : r + 1], st, et)


def corner_edges(cin, st, et):
    for i, R in enumerate((0, ROWS_DEV + 1)):
        both = cin[i].astype(jnp.float32)
        place_edges(R, both[0:1], both[1:2], st, et)
    et[20:32, :] = jnp.zeros((12, DEPTH), jnp.float32)


def pair_product(d, st, p, i, j):
    a = pl.multiple_of(LEAD + 16 + PITCH * i, 16)
    b = pl.multiple_of(LEAD + 16 + PITCH * j, 16)
    rows = jnp.concatenate([st[pl.ds(a, 128), :], st[pl.ds(b, 128), :]], axis=0)
    out = lax.dot_general(d[...].reshape(1024, DEPTH), rows, NT, preferred_element_type=jnp.float32)
    p[i] = out[:, :128]
    p[j] = out[:, 128:]


def own_products(d, st, p):
    def pair(i, carry):
        pair_product(d, st, p, 2 * i + 1, 2 * i + 2)
        return carry

    lax.fori_loop(0, ROWS_DEV // 2, pair, 0)


def edge_products(d, st, et, p):
    pair_product(d, st, p, 0, ROWS_DEV + 1)
    edge = et[...].astype(jnp.bfloat16)
    edge = jnp.concatenate([edge, jnp.zeros((96, DEPTH), jnp.bfloat16)], axis=0)
    p[10] = lax.dot_general(d[...].reshape(1024, DEPTH), edge, NT, preferred_element_type=jnp.float32)


def entry_norms(d, inv):
    tail = d[:, :, :, DEPTH - 128 :].reshape(1024, 128).astype(jnp.float32)
    at = RUN - 128
    value = tail[:, at : at + 1] + tail[:, at + 1 : at + 2] + tail[:, at + 2 : at + 3]
    inv[...] = jnp.broadcast_to(value, inv.shape)


def edge_mix(p, we):
    def step(k, carry):
        at = pl.ds(pl.multiple_of(k * 8, 8), 8)
        e = p[10, at, :]
        mix = e * we[1:2, :] + pltpu.roll(e, 2, 1) * we[0:1, :] + pltpu.roll(e, 126, 1) * we[2:3, :]
        p[10, at, :] = mix
        return carry

    lax.fori_loop(0, 128, step, 0, unroll=8)


def best_scores(p, inv, wc, o_ref):
    lane = lax.broadcasted_iota(jnp.int32, (8, 128), 1)
    first, last = lane == 0, lane == 127
    for r in range(ROWS_DEV):
        wt = [jnp.broadcast_to(wc[r, kk : kk + 1, :], (8, 128)) for kk in range(9)]
        R = r + 1

        def step(k, best):
            at = pl.ds(pl.multiple_of(k * 8, 8), 8)
            up, mid, down = p[r, at, :], p[r + 1, at, :], p[r + 2, at, :]
            edge = pltpu.roll(p[10, at, :], 127 - 2 * R, 1)
            left = up * wt[0] + mid * wt[3] + down * wt[6]
            right = up * wt[2] + mid * wt[5] + down * wt[8]
            here = up * wt[1] + mid + down * wt[7]
            left = jnp.where(last, edge, left)
            right = jnp.where(first, edge, right)
            v = (here + pltpu.roll(left, 1, 1) + pltpu.roll(right, 127, 1)) * inv[at, :]
            b0, b1, b2, b3 = best
            n0, v = jnp.maximum(b0, v), jnp.minimum(b0, v)
            n1, v = jnp.maximum(b1, v), jnp.minimum(b1, v)
            n2, v = jnp.maximum(b2, v), jnp.minimum(b2, v)
            return n0, n1, n2, jnp.maximum(b3, v)

        low = jnp.full((8, 128), -jnp.inf, jnp.float32)
        best = lax.fori_loop(0, 128, step, (low, low, low, low), unroll=4)
        for shift in (6, 7):
            other = [pltpu.roll(b, shift, 0) for b in best]
            m = [jnp.maximum(best[i], other[3 - i]) for i in range(4)]
            h0, l0 = jnp.maximum(m[0], m[2]), jnp.minimum(m[0], m[2])
            h1, l1 = jnp.maximum(m[1], m[3]), jnp.minimum(m[1], m[3])
            best = (jnp.maximum(h0, h1), jnp.minimum(h0, h1), jnp.maximum(l0, l1), jnp.minimum(l0, l1))
        scale = wc[r, 9:10, :]
        for j in range(TOP):
            o_ref[0, j, r : r + 1, :] = best[j][0:1] * scale
            o_ref[1, j, r : r + 1, :] = best[j][4:5] * scale


def send(src, dst, sems, i, device):
    return pltpu.make_async_remote_copy(
        src_ref=src,
        dst_ref=dst,
        send_sem=sems.at[0, i],
        recv_sem=sems.at[1, i],
        device_id=device,
        device_id_type=pl.DeviceIdType.MESH,
    )


COPIES = 48


def index_kernel(x_hbm, k1_ref, k2_ref, eye_ref, order_ref, m_ref, nm_ref, dict_ref, o_ref,
                 xbuf, xs, h, c, d, own, sib, st, eout, ein, cout, cin,
                 et, p, f8, u, w, wc, we, inv, xsem, sems):
    strip, slot = lax.axis_index("strip"), lax.axis_index("dict")
    core, zl = slot % 2, slot // 2
    zh, ix, iy = strip // 16, (strip // 4) % 4, strip % 4
    iz = zh * 2 + zl

    def chip(x, y, z):
        x, y, z = x % 4, y % 4, z % 4
        return ((z // 2) * 16 + x * 4 + y, (z % 2) * 2 + core)

    sibling = (strip, zl * 2 + (1 - core))
    x_up, x_down = chip(ix + 1, iy, iz), chip(ix + 3, iy, iz)
    y_up, y_down = chip(ix, iy + 1, iz), chip(ix, iy + 3, iz)
    z_up, z_down = chip(ix, iy, iz + 1), chip(ix, iy, iz + 3)
    row_up, row_down = ((strip + 31) % 32, slot), ((strip + 1) % 32, slot)
    col_left, col_right = (strip, (slot + 3) % 4), (strip, (slot + 1) % 4)

    def fetch(g, at):
        rows = pl.ds(pl.multiple_of(g * RUN, RUN), RUN)
        return pltpu.make_async_copy(x_hbm.at[rows], xbuf.at[at], xsem.at[at])

    fetch(0, 0).start()
    peers = (sibling, x_up, x_down, y_up, y_down, z_up, z_down, row_up, row_down, col_left, col_right)
    barrier = pltpu.get_barrier_semaphore()
    for peer in peers:
        pl.semaphore_signal(barrier, inc=1, device_id=peer, device_id_type=pl.DeviceIdType.MESH)
    prepare(dict_ref, order_ref, own)
    pl.semaphore_wait(barrier, len(peers))
    exchange = send(own, sib, sems, 0, sibling)
    exchange.start()

    base = pl.multiple_of(core * 1920, 128)
    half = pl.ds(base, 1920)
    part_a = pl.ds(base, 1024)
    part_b = pl.ds(pl.multiple_of(base + 1024, 128), 896)
    xu, xd, yu, yd, zu, zd = [(v % 4) for v in (ix + 1, ix + 3, iy + 1, iy + 3, iz + 1, iz + 3)]

    def same(ref, i, device):
        return send(ref, ref, sems, i, device)

    def rows_of(y):
        return pl.ds(pl.multiple_of(y * 16, 16), 16)

    upper, lower = pl.ds(0, 32), pl.ds(32, 32)
    y_first = [same(d.at[ix, iz, rows_of(iy), half], 1, y_up), same(d.at[ix, iz, rows_of(iy), half], 2, y_down)]
    y_second = [same(d.at[ix, iz, rows_of(yd), part_a], 3, y_up), same(d.at[ix, iz, rows_of(yu), part_b], 4, y_down)]
    mid_first = [
        same(d.at[ix, iz, :, part_a], 5, z_up),
        same(d.at[ix, iz, :, part_a], 6, z_down),
        same(d.at[ix, iz, :, part_b], 7, x_up),
        same(d.at[ix, iz, :, part_b], 8, x_down),
    ]
    mid_second = [
        same(d.at[ix, zd, upper, part_a], 9, z_up),
        same(d.at[ix, zu, lower, part_a], 10, z_down),
        same(d.at[xd, iz, upper, part_b], 11, x_up),
        same(d.at[xu, iz, lower, part_b], 12, x_down),
    ]
    last_first = [
        same(d.at[ix, :, :, part_a], 13, x_up),
        same(d.at[ix, :, :, part_a], 14, x_down),
        same(d.at[:, iz, :, part_b], 15, z_up),
        same(d.at[:, iz, :, part_b], 16, z_down),
        same(d.at[ix, :, :, part_a], 17, sibling),
        same(d.at[:, iz, :, part_b], 18, sibling),
    ]
    first_two, last_two = pl.ds(0, 2), pl.ds(2, 2)
    last_second = [
        same(d.at[xd, first_two, :, part_a], 19, x_up),
        same(d.at[xu, last_two, :, part_a], 20, x_down),
        same(d.at[first_two, zd, :, part_b], 21, z_up),
        same(d.at[last_two, zu, :, part_b], 22, z_down),
        same(d.at[xd, :, :, part_a], 23, sibling),
        same(d.at[xu, :, :, part_a], 24, sibling),
        same(d.at[:, zd, :, part_b], 25, sibling),
        same(d.at[:, zu, :, part_b], 26, sibling),
    ]
    xo, zo = (ix + 2) % 4, (iz + 2) % 4
    final = [
        same(d.at[xo, :, :, part_a], 27, sibling),
        same(d.at[:, zo, :, part_b], 28, sibling),
    ]

    def start(copies):
        for copy in copies:
            copy.start()

    def arrive(copies):
        for copy in copies:
            copy.wait_recv()

    def begin():
        exchange.wait_recv()
        mine, other = own[:, half], sib[:, half]
        first = core == 0
        both = jnp.concatenate([jnp.where(first, mine, other), jnp.where(first, other, mine)], axis=0)
        d[ix, iz, rows_of(iy), half] = both.astype(jnp.bfloat16)
        start(y_first)

    def forward(arrived, following):
        def act():
            arrive(arrived)
            start(following)
        return act

    events = {
        1: begin,
        3: forward(y_first, y_second),
        5: forward(y_second, mid_first),
        8: forward(mid_first, mid_second),
        10: forward(mid_second, last_first),
    }
    st[pl.ds(0, LEAD), :] = jnp.zeros((LEAD, DEPTH), jnp.bfloat16)
    tail = LANES - 10 * PITCH
    st[pl.ds(LEAD + 10 * PITCH, tail), :] = jnp.zeros((tail, DEPTH), jnp.bfloat16)
    w[...] = jnp.zeros_like(w)
    usable_rows(nm_ref, u, strip * ROWS_DEV, slot * COLS_DEV, 32 * ROWS_DEV, 4 * COLS_DEV)

    def chunk(g, carry):
        at = g % 2

        @pl.when(g + 1 < GROUPS)
        def _():
            fetch(g + 1, 1 - at).start()

        fetch(g, at).wait()
        first_pass(g, xbuf.at[at], k1_ref, xs, h, c)
        for when, act in events.items():
            pl.when(g == when)(act)
        return carry

    lax.fori_loop(0, GROUPS, chunk, 0)

    row_copies = [
        send(st.at[pl.ds(own_start(7), 128), :], st.at[pl.ds(own_start(-1), 128), :], sems, 29, row_down),
        send(st.at[pl.ds(own_start(0), 128), :], st.at[pl.ds(own_start(8), 128), :], sems, 30, row_up),
    ]
    edge_copies = [
        send(eout.at[0], ein.at[1], sems, 31, col_left),
        send(eout.at[1], ein.at[0], sems, 32, col_right),
    ]
    corner_copies = [
        send(cout.at[0], cin.at[1], sems, 33, row_up),
        send(cout.at[1], cin.at[0], sems, 34, row_down),
    ]
    second_pass(3, k2_ref, eye_ref, m_ref, h, c, st)
    row_copies[0].start()
    second_pass(0, k2_ref, eye_ref, m_ref, h, c, st)
    row_copies[1].start()
    forward(last_first, last_second)()
    second_pass(1, k2_ref, eye_ref, m_ref, h, c, st)
    second_pass(2, k2_ref, eye_ref, m_ref, h, c, st)
    own_edges(st, et, eout)
    start(edge_copies)
    forward(last_second, final)()
    arrive(edge_copies)
    inner_edges(ein, st, et, cout)
    start(corner_copies)
    arrive(final)
    entry_norms(d, inv)
    own_products(d, st, p)
    arrive(corner_copies)
    corner_edges(cin, st, et)
    arrive(row_copies)
    edge_products(d, st, et, p)
    gram_fields(st, f8)
    weigh(f8, u, w)
    spread(w, wc, we)
    edge_mix(p, we)
    best_scores(p, inv, wc, o_ref)
    everything = [exchange] + y_first + y_second + mid_first + mid_second + last_first + last_second + final
    for copy in everything + row_copies + edge_copies + corner_copies:
        copy.wait_send()


def on_device(patterns, scan_mask, neighbour_mask, dictionary):
    k1, k2, eye, order_t = tables()
    vmem = pl.BlockSpec(memory_space=pltpu.VMEM)
    bf, f32 = jnp.bfloat16, jnp.float32
    return pl.pallas_call(
        index_kernel,
        in_specs=[pl.BlockSpec(memory_space=pl.ANY)] + [vmem] * 7,
        out_specs=vmem,
        out_shape=jax.ShapeDtypeStruct((2, TOP, ROWS_DEV, COLS_DEV), f32),
        scratch_shapes=[
            pltpu.VMEM((2, RUN, ROWS_DEV, COLS_DEV), bf),
            pltpu.VMEM((RUN * 8, 128), f32),
            pltpu.VMEM((4, GROUPS, RUN, 256), bf),
            pltpu.VMEM((4, GROUPS, GROUPS, 16, 256), f32),
            pltpu.VMEM((4, 4, 64, DEPTH), bf),
            pltpu.VMEM((8, DEPTH), f32),
            pltpu.VMEM((8, DEPTH), f32),
            pltpu.VMEM((HELD, DEPTH), bf),
            pltpu.VMEM((2, 16, DEPTH), bf),
            pltpu.VMEM((2, 16, DEPTH), bf),
            pltpu.VMEM((2, 16, DEPTH), bf),
            pltpu.VMEM((2, 16, DEPTH), bf),
            pltpu.VMEM((32, DEPTH), f32),
            pltpu.VMEM((11, 1024, 128), f32),
            pltpu.VMEM((9, 8, LANES), f32),
            pltpu.VMEM((8, LANES), f32),
            pltpu.VMEM((16, LANES), f32),
            pltpu.VMEM((8, 16, 128), f32),
            pltpu.VMEM((8, 128), f32),
            pltpu.VMEM((1024, 128), f32),
            pltpu.SemaphoreType.DMA((2,)),
            pltpu.SemaphoreType.DMA((2, COPIES)),
        ],
        compiler_params=pltpu.CompilerParams(
            vmem_limit_bytes=67_043_328, collective_id=0, has_side_effects=True
        ),
        name="index",
    )(patterns, k1, k2, eye, order_t, scan_mask, neighbour_mask, dictionary)


def solution(mesh):
    in_specs = (
        P(None, "strip", "dict"),
        P("strip", "dict"),
        P(None, "strip", "dict"),
        P(None, ("strip", "dict"), None),
    )
    out_specs = P(None, None, "strip", "dict")
    return jax.shard_map(
        on_device, mesh=mesh, in_specs=in_specs, out_specs=out_specs, check_vma=False
    )
```

time: 247 us -> 141 us (0.57)
  waiting for transfers between devices: 89.6 us -> 0 us
  Pallas kernels: 117 us -> 139 us
  between operations: 13.4 us -> 0.01 us
  starting transfers between devices: 10.4 us -> 0 us
  blocking collectives: 9.42 us -> 0 us
    ppermute x4 -> x0, waiting for transfers between devices: 76.5 us -> none  [shift(): lax.ppermute(value, axis, [(i, (i + step) % count) for i in range(count)])]
    pallas_call x3 -> x1, Pallas kernels: 117 us -> 139 us  [on_device(): pl.pallas_call(index_kernel, in_specs=[pl.BlockSpec(memory_space=pl.ANY)]...]
    all_gather x1 -> x0, waiting for transfers between devices: 13.2 us -> none  [gather_entries(): lax.all_gather(grouped.reshape(-1, DEPTH), 'strip', axis=0, tiled=True)]
    ppermute x4 -> x0, starting transfers between devices: 10.4 us -> none  [shift(): lax.ppermute(value, axis, [(i, (i + step) % count) for i in range(count)])]
    all_to_all x1 -> x0, blocking collectives: 9.42 us -> none  [gather_entries(): lax.all_to_all(copies, 'dict', split_axis=0, concat_axis=0, tiled=True)]
  transfers between devices with their start and end apart: 5 -> 0, of which waited for: 4 -> 0; matrix products, arithmetic and copies ran while one was open for 2% -> 0% of each run, Pallas kernels for 17% -> 0%
where the time goes in v1:
time: 141 us
  Pallas kernels  139 us (99%)
    pallas_call x1, Pallas kernels, on_device(): pl.pallas_call(index_kernel, in_specs=[pl.BlockSpec(memory_space=pl.ANY)]...  139 us

profile of v1, /device:TPU:1, one launch (start us, length us, event | category | flops | bytes accessed | tf_op | source)
XLA Modules:
  0.0 140.7 jit_solution(15122776943910072158)
XLA Ops:
  0.0 139.3 %index.1 = f32[2,4,8,128]{3,2,1,0:T(8,128)} custom-call(bf16[3600,8,128]{2,1,0:T(8,128)(2,1)} %x_hbm.1, bf16[480,240]{1,0:T(8,128)(2,1)} %constant.8.clone.k1_ref, bf16[240,240]{1,0:T(8,128)(2,1)} %constant.9.clone.k2_ref, bf16[256,256]{1,0:T(8,128)(2,1)} %constant.10.clone.eye_ref, bf16[240,256]{1,0:T(8,128)(2,1)} %constant.11.clone.order_ref, ...), custom_call_target="tpu_custom_call" | custom-call | tf_op jit(solution)/shard_map/index/pallas_call | solution.py:528
  139.3 1.4 copy.10

commit v2 on v1

--- a/solution.py
+++ b/solution.py
@@ -68,7 +68,8 @@
 
 def first_pass(g, x_ref, k1_ref, xs, h, c):
     for j in range(6):
-        xs[pl.ds(j * 320, 320), :] = x_ref[pl.ds(j * 40, 40)].astype(jnp.float32).reshape(320, 128)
+        part = x_ref[pl.ds(j * 40, 40)].astype(jnp.float32)
+        xs[pl.ds(j * 320, 320), :] = part.reshape(320, 128)
     h_at = pl.ds(pl.multiple_of(g * 16, 16), 16)
     for n in range(4):
         even = xs[pl.ds(2 * n, RUN, stride=8), :].astype(jnp.bfloat16)
@@ -89,7 +90,7 @@
         return total + jnp.sum(part, axis=0), square + jnp.sum(part * part, axis=0)
 
     zero = jnp.zeros((8, 256), jnp.float32)
-    total, square = lax.fori_loop(0, GROUPS, second, (zero, zero))
+    total, square = lax.fori_loop(0, GROUPS, second, (zero, zero), unroll=15)
     mean = jnp.sum(total, axis=0, keepdims=True) / NPIX
     var = jnp.sum(square, axis=0, keepdims=True) / NPIX - mean * mean
     mask = jnp.concatenate([m_ref[2 * n : 2 * n + 1, :], m_ref[2 * n + 1 : 2 * n + 2, :]], axis=1)
@@ -106,7 +107,7 @@
         st[pl.ds(own_start(2 * n + 1), 128), at] = out[128:]
         return carry
 
-    lax.fori_loop(0, GROUPS, third, 0)
+    lax.fori_loop(0, GROUPS, third, 0, unroll=15)
 
 
 def row_start(scan_row):
@@ -117,17 +118,16 @@
     return row_start(r + 1) + 16
 
 
-def gram_fields(st, f8):
+def gram_fields(st, f8, begin, end, tile_of):
     row_at = lax.broadcasted_iota(jnp.int32, (136, 128), 0)
     lane_at = lax.broadcasted_iota(jnp.int32, (136, 128), 1)
     slots = {}
     for kk in range(9):
         for low in range(min(kk + 1, 8)):
             slots.setdefault(OFFSETS[kk] - OFFSETS[low], []).append((kk, low))
-    f8[...] = jnp.zeros_like(f8)
-
-    def tile(t, carry):
-        n0 = pl.multiple_of(t * 256, 256)
+
+    def tile(i, carry):
+        n0 = pl.multiple_of(tile_of(i) * 256, 256)
         rows = st[pl.ds(n0, LEAD + 256), :]
         cols = st[pl.ds(pl.multiple_of(n0 + LEAD, 16), 256), :]
         g = lax.dot_general(rows, cols, NT, preferred_element_type=jnp.float32)
@@ -143,7 +143,7 @@
                     f8[kk, low : low + 1, at] = value
         return carry
 
-    lax.fori_loop(0, TILES, tile, 0)
+    lax.fori_loop(begin, end, tile, 0)
 
 
 def usable_rows(nm_ref, u, first_row, first_col, all_rows, all_cols):
@@ -293,41 +293,58 @@
     lax.fori_loop(0, 128, step, 0, unroll=8)
 
 
+def order(x, i, j):
+    x[i], x[j] = jnp.maximum(x[i], x[j]), jnp.minimum(x[i], x[j])
+
+
+def merge_best(best, other):
+    m = [jnp.maximum(best[i], other[3 - i]) for i in range(4)]
+    for i, j in ((0, 2), (1, 3), (0, 1), (2, 3)):
+        order(m, i, j)
+    return m
+
+
+STEP = 32
+
+
 def best_scores(p, inv, wc, o_ref):
     lane = lax.broadcasted_iota(jnp.int32, (8, 128), 1)
     first, last = lane == 0, lane == 127
-    for r in range(ROWS_DEV):
+
+    def scan_row(r, carry):
         wt = [jnp.broadcast_to(wc[r, kk : kk + 1, :], (8, 128)) for kk in range(9)]
-        R = r + 1
-
-        def step(k, best):
-            at = pl.ds(pl.multiple_of(k * 8, 8), 8)
+        turn = 125 - 2 * r
+
+        def score(at):
             up, mid, down = p[r, at, :], p[r + 1, at, :], p[r + 2, at, :]
-            edge = pltpu.roll(p[10, at, :], 127 - 2 * R, 1)
+            edge = pltpu.roll(p[10, at, :], turn, 1)
             left = up * wt[0] + mid * wt[3] + down * wt[6]
             right = up * wt[2] + mid * wt[5] + down * wt[8]
             here = up * wt[1] + mid + down * wt[7]
             left = jnp.where(last, edge, left)
             right = jnp.where(first, edge, right)
-            v = (here + pltpu.roll(left, 1, 1) + pltpu.roll(right, 127, 1)) * inv[at, :]
-            b0, b1, b2, b3 = best
-            n0, v = jnp.maximum(b0, v), jnp.minimum(b0, v)
-            n1, v = jnp.maximum(b1, v), jnp.minimum(b1, v)
-            n2, v = jnp.maximum(b2, v), jnp.minimum(b2, v)
-            return n0, n1, n2, jnp.maximum(b3, v)
+            return (here + pltpu.roll(left, 1, 1) + pltpu.roll(right, 127, 1)) * inv[at, :]
+
+        def step(k, best):
+            best = list(best)
+            for i in range(0, STEP, 4):
+                v = [score(pl.ds(pl.multiple_of(k * (8 * STEP) + (i + j) * 8, 8), 8)) for j in range(4)]
+                for a, b in ((0, 1), (2, 3), (0, 2), (1, 3), (1, 2)):
+                    order(v, a, b)
+                best = merge_best(best, v)
+            return tuple(best)
 
         low = jnp.full((8, 128), -jnp.inf, jnp.float32)
-        best = lax.fori_loop(0, 128, step, (low, low, low, low), unroll=4)
+        best = lax.fori_loop(0, 128 // STEP, step, (low, low, low, low))
         for shift in (6, 7):
-            other = [pltpu.roll(b, shift, 0) for b in best]
-            m = [jnp.maximum(best[i], other[3 - i]) for i in range(4)]
-            h0, l0 = jnp.maximum(m[0], m[2]), jnp.minimum(m[0], m[2])
-            h1, l1 = jnp.maximum(m[1], m[3]), jnp.minimum(m[1], m[3])
-            best = (jnp.maximum(h0, h1), jnp.minimum(h0, h1), jnp.maximum(l0, l1), jnp.minimum(l0, l1))
+            best = merge_best(best, [pltpu.roll(b, shift, 0) for b in best])
         scale = wc[r, 9:10, :]
         for j in range(TOP):
-            o_ref[0, j, r : r + 1, :] = best[j][0:1] * scale
-            o_ref[1, j, r : r + 1, :] = best[j][4:5] * scale
+            o_ref[0, j, pl.ds(r, 1), :] = best[j][0:1] * scale
+            o_ref[1, j, pl.ds(r, 1), :] = best[j][4:5] * scale
+        return carry
+
+    lax.fori_loop(0, ROWS_DEV, scan_row, 0)
 
 
 def send(src, dst, sems, i, device):
@@ -342,6 +359,7 @@
 
 
 COPIES = 48
+BATCH = 3
 
 
 def index_kernel(x_hbm, k1_ref, k2_ref, eye_ref, order_ref, m_ref, nm_ref, dict_ref, o_ref,
@@ -364,7 +382,7 @@
     col_left, col_right = (strip, (slot + 3) % 4), (strip, (slot + 1) % 4)
 
     def fetch(g, at):
-        rows = pl.ds(pl.multiple_of(g * RUN, RUN), RUN)
+        rows = pl.ds(pl.multiple_of(g * (BATCH * RUN), BATCH * RUN), BATCH * RUN)
         return pltpu.make_async_copy(x_hbm.at[rows], xbuf.at[at], xsem.at[at])
 
     fetch(0, 0).start()
@@ -452,32 +470,33 @@
         return act
 
     events = {
-        1: begin,
-        3: forward(y_first, y_second),
-        5: forward(y_second, mid_first),
-        8: forward(mid_first, mid_second),
-        10: forward(mid_second, last_first),
+        0: begin,
+        1: forward(y_first, y_second),
+        2: forward(y_second, mid_first),
+        4: forward(mid_first, mid_second),
     }
     st[pl.ds(0, LEAD), :] = jnp.zeros((LEAD, DEPTH), jnp.bfloat16)
     tail = LANES - 10 * PITCH
     st[pl.ds(LEAD + 10 * PITCH, tail), :] = jnp.zeros((tail, DEPTH), jnp.bfloat16)
     w[...] = jnp.zeros_like(w)
+    f8[...] = jnp.zeros_like(f8)
     usable_rows(nm_ref, u, strip * ROWS_DEV, slot * COLS_DEV, 32 * ROWS_DEV, 4 * COLS_DEV)
 
     def chunk(g, carry):
         at = g % 2
 
-        @pl.when(g + 1 < GROUPS)
+        @pl.when(g + 1 < GROUPS // BATCH)
         def _():
             fetch(g + 1, 1 - at).start()
 
         fetch(g, at).wait()
-        first_pass(g, xbuf.at[at], k1_ref, xs, h, c)
+        for i in range(BATCH):
+            first_pass(g * BATCH + i, xbuf.at[at, pl.ds(i * RUN, RUN)], k1_ref, xs.at[i], h, c)
         for when, act in events.items():
             pl.when(g == when)(act)
         return carry
 
-    lax.fori_loop(0, GROUPS, chunk, 0)
+    lax.fori_loop(0, GROUPS // BATCH, chunk, 0)
 
     row_copies = [
         send(st.at[pl.ds(own_start(7), 128), :], st.at[pl.ds(own_start(-1), 128), :], sems, 29, row_down),
@@ -495,25 +514,27 @@
     row_copies[0].start()
     second_pass(0, k2_ref, eye_ref, m_ref, h, c, st)
     row_copies[1].start()
-    forward(last_first, last_second)()
+    forward(mid_second, last_first)()
     second_pass(1, k2_ref, eye_ref, m_ref, h, c, st)
     second_pass(2, k2_ref, eye_ref, m_ref, h, c, st)
     own_edges(st, et, eout)
     start(edge_copies)
-    forward(last_second, final)()
     arrive(edge_copies)
     inner_edges(ein, st, et, cout)
     start(corner_copies)
+    gram_fields(st, f8, 2, 5, lambda i: i)
+    forward(last_first, last_second)()
+    arrive(corner_copies)
+    corner_edges(cin, st, et)
+    forward(last_second, final)()
+    arrive(row_copies)
+    gram_fields(st, f8, 0, 4, lambda i: i + 3 * (i // 2))
+    weigh(f8, u, w)
+    spread(w, wc, we)
     arrive(final)
     entry_norms(d, inv)
     own_products(d, st, p)
-    arrive(corner_copies)
-    corner_edges(cin, st, et)
-    arrive(row_copies)
     edge_products(d, st, et, p)
-    gram_fields(st, f8)
-    weigh(f8, u, w)
-    spread(w, wc, we)
     edge_mix(p, we)
     best_scores(p, inv, wc, o_ref)
     everything = [exchange] + y_first + y_second + mid_first + mid_second + last_first + last_second + final
@@ -531,8 +552,8 @@
         out_specs=vmem,
         out_shape=jax.ShapeDtypeStruct((2, TOP, ROWS_DEV, COLS_DEV), f32),
         scratch_shapes=[
-            pltpu.VMEM((2, RUN, ROWS_DEV, COLS_DEV), bf),
-            pltpu.VMEM((RUN * 8, 128), f32),
+            pltpu.VMEM((2, BATCH * RUN, ROWS_DEV, COLS_DEV), bf),
+            pltpu.VMEM((BATCH, RUN * 8, 128), f32),
             pltpu.VMEM((4, GROUPS, RUN, 256), bf),
             pltpu.VMEM((4, GROUPS, GROUPS, 16, 256), f32),
             pltpu.VMEM((4, 4, 64, DEPTH), bf),

time: 141 us -> 101 us (0.72)
  Pallas kernels: 139 us -> 99.8 us
    pallas_call x1, Pallas kernels: 139 us -> 99.8 us  [on_device(): pl.pallas_call(index_kernel, in_specs=[pl.BlockSpec(memory_space=pl.ANY)]...]
where the time goes in v2:
time: 101 us
  Pallas kernels  99.8 us (99%)
  local copies, waits for them, and re-layouts  1.38 us (1%)
    pallas_call x1, Pallas kernels, on_device(): pl.pallas_call(index_kernel, in_specs=[pl.BlockSpec(memory_space=pl.ANY)]...  99.8 us

profile of v2, /device:TPU:1, one launch (start us, length us, event | category | flops | bytes accessed | tf_op | source)
XLA Modules:
  0.0 101.2 jit_solution(11017564633354993344)
XLA Ops:
  0.0 99.8 %index.1 = f32[2,4,8,128]{3,2,1,0:T(8,128)} custom-call(bf16[3600,8,128]{2,1,0:T(8,128)(2,1)} %x_hbm.1, bf16[480,240]{1,0:T(8,128)(2,1)} %constant.8.clone.k1_ref, bf16[240,240]{1,0:T(8,128)(2,1)} %constant.9.clone.k2_ref, bf16[256,256]{1,0:T(8,128)(2,1)} %constant.10.clone.eye_ref, bf16[240,256]{1,0:T(8,128)(2,1)} %constant.11.clone.order_ref, ...), custom_call_target="tpu_custom_call" | custom-call | tf_op jit(solution)/shard_map/index/pallas_call | solution.py:549
  99.8 1.4 %copy.10 = f32[2,4,8,128]{3,2,1,0:T(8,128)} copy(f32[2,4,8,128]{3,2,1,0:T(8,128)} %index.1) | data formatting | bytes 65536

commit v3 on v2

--- a/solution.py
+++ b/solution.py
@@ -276,7 +276,7 @@
 
 
 def entry_norms(d, inv):
-    tail = d[:, :, :, DEPTH - 128 :].reshape(1024, 128).astype(jnp.float32)
+    tail = d[:, :, :, :, DEPTH - 128 :].reshape(1024, 128).astype(jnp.float32)
     at = RUN - 128
     value = tail[:, at : at + 1] + tail[:, at + 1 : at + 2] + tail[:, at + 2 : at + 3]
     inv[...] = jnp.broadcast_to(value, inv.shape)
@@ -290,7 +290,7 @@
         p[10, at, :] = mix
         return carry
 
-    lax.fori_loop(0, 128, step, 0, unroll=8)
+    lax.fori_loop(0, 128, step, 0, unroll=16)
 
 
 def order(x, i, j):
@@ -358,7 +358,7 @@
     )
 
 
-COPIES = 48
+COPIES = 64
 BATCH = 3
 
 
@@ -391,61 +391,45 @@
     for peer in peers:
         pl.semaphore_signal(barrier, inc=1, device_id=peer, device_id_type=pl.DeviceIdType.MESH)
     prepare(dict_ref, order_ref, own)
-    pl.semaphore_wait(barrier, len(peers))
     exchange = send(own, sib, sems, 0, sibling)
-    exchange.start()
 
     base = pl.multiple_of(core * 1920, 128)
     half = pl.ds(base, 1920)
-    part_a = pl.ds(base, 1024)
-    part_b = pl.ds(pl.multiple_of(base + 1024, 128), 896)
-    xu, xd, yu, yd, zu, zd = [(v % 4) for v in (ix + 1, ix + 3, iy + 1, iy + 3, iz + 1, iz + 3)]
-
-    def same(ref, i, device):
-        return send(ref, ref, sems, i, device)
-
-    def rows_of(y):
-        return pl.ds(pl.multiple_of(y * 16, 16), 16)
-
-    upper, lower = pl.ds(0, 32), pl.ds(32, 32)
-    y_first = [same(d.at[ix, iz, rows_of(iy), half], 1, y_up), same(d.at[ix, iz, rows_of(iy), half], 2, y_down)]
-    y_second = [same(d.at[ix, iz, rows_of(yd), part_a], 3, y_up), same(d.at[ix, iz, rows_of(yu), part_b], 4, y_down)]
-    mid_first = [
-        same(d.at[ix, iz, :, part_a], 5, z_up),
-        same(d.at[ix, iz, :, part_a], 6, z_down),
-        same(d.at[ix, iz, :, part_b], 7, x_up),
-        same(d.at[ix, iz, :, part_b], 8, x_down),
-    ]
-    mid_second = [
-        same(d.at[ix, zd, upper, part_a], 9, z_up),
-        same(d.at[ix, zu, lower, part_a], 10, z_down),
-        same(d.at[xd, iz, upper, part_b], 11, x_up),
-        same(d.at[xu, iz, lower, part_b], 12, x_down),
-    ]
-    last_first = [
-        same(d.at[ix, :, :, part_a], 13, x_up),
-        same(d.at[ix, :, :, part_a], 14, x_down),
-        same(d.at[:, iz, :, part_b], 15, z_up),
-        same(d.at[:, iz, :, part_b], 16, z_down),
-        same(d.at[ix, :, :, part_a], 17, sibling),
-        same(d.at[:, iz, :, part_b], 18, sibling),
-    ]
-    first_two, last_two = pl.ds(0, 2), pl.ds(2, 2)
-    last_second = [
-        same(d.at[xd, first_two, :, part_a], 19, x_up),
-        same(d.at[xu, last_two, :, part_a], 20, x_down),
-        same(d.at[first_two, zd, :, part_b], 21, z_up),
-        same(d.at[last_two, zu, :, part_b], 22, z_down),
-        same(d.at[xd, :, :, part_a], 23, sibling),
-        same(d.at[xu, :, :, part_a], 24, sibling),
-        same(d.at[:, zd, :, part_b], 25, sibling),
-        same(d.at[:, zu, :, part_b], 26, sibling),
-    ]
-    xo, zo = (ix + 2) % 4, (iz + 2) % 4
-    final = [
-        same(d.at[xo, :, :, part_a], 27, sibling),
-        same(d.at[:, zo, :, part_b], 28, sibling),
-    ]
+    mine = {"x": ix, "y": iy, "z": iz}
+    ring = {"x": (x_up, x_down), "y": (y_up, y_down), "z": (z_up, z_down)}
+    count = iter(range(1, 64))
+
+    def region(lanes, **at):
+        where = {axis: at.get(axis, pl.ds(0, 4)) for axis in "xyz"}
+        return d.at[where["x"], where["z"], where["y"], :, lanes]
+
+    def same(ref, device):
+        return send(ref, ref, sems, next(count), device)
+
+    firsts, seconds = ([], [], []), ([], [], [])
+    shared = ([], [], [])
+    for part, order_of in enumerate(("yzx", "zxy", "xyz")):
+        begin_at = base + 640 * part
+        lanes = pl.ds(pl.multiple_of(begin_at, 128), 640)
+        ahead = pl.ds(pl.multiple_of(begin_at, 128), 384)
+        behind = pl.ds(pl.multiple_of(begin_at + 384, 128), 256)
+        for phase, axis in enumerate(order_of):
+            at = {other: mine[other] for other in order_of[phase + 1 :]}
+            up, down = ring[axis]
+            here, after, before = mine[axis], (mine[axis] + 1) % 4, (mine[axis] + 3) % 4
+            block = region(lanes, **at, **{axis: here})
+            firsts[phase].extend((same(block, up), same(block, down)))
+            seconds[phase].append(same(region(ahead, **at, **{axis: before}), up))
+            seconds[phase].append(same(region(behind, **at, **{axis: after}), down))
+            if phase == 2:
+                shared[0].append(same(block, sibling))
+                shared[1].append(same(region(lanes, **{axis: before}), sibling))
+                shared[1].append(same(region(lanes, **{axis: after}), sibling))
+                shared[2].append(same(region(lanes, **{axis: (here + 2) % 4}), sibling))
+    stages = (
+        firsts[0], seconds[0], firsts[1], seconds[1],
+        firsts[2] + shared[0], seconds[2] + shared[1], shared[2],
+    )
 
     def start(copies):
         for copy in copies:
@@ -457,24 +441,16 @@
 
     def begin():
         exchange.wait_recv()
-        mine, other = own[:, half], sib[:, half]
+        ours, theirs = own[:, half], sib[:, half]
         first = core == 0
-        both = jnp.concatenate([jnp.where(first, mine, other), jnp.where(first, other, mine)], axis=0)
-        d[ix, iz, rows_of(iy), half] = both.astype(jnp.bfloat16)
-        start(y_first)
-
-    def forward(arrived, following):
-        def act():
-            arrive(arrived)
-            start(following)
-        return act
-
-    events = {
-        0: begin,
-        1: forward(y_first, y_second),
-        2: forward(y_second, mid_first),
-        4: forward(mid_first, mid_second),
-    }
+        both = jnp.concatenate([jnp.where(first, ours, theirs), jnp.where(first, theirs, ours)], axis=0)
+        d[ix, iz, iy, :, half] = both.astype(jnp.bfloat16)
+        start(stages[0])
+
+    def forward(stage):
+        arrive(stages[stage - 1])
+        start(stages[stage])
+
     st[pl.ds(0, LEAD), :] = jnp.zeros((LEAD, DEPTH), jnp.bfloat16)
     tail = LANES - 10 * PITCH
     st[pl.ds(LEAD + 10 * PITCH, tail), :] = jnp.zeros((tail, DEPTH), jnp.bfloat16)
@@ -492,53 +468,60 @@
         fetch(g, at).wait()
         for i in range(BATCH):
             first_pass(g * BATCH + i, xbuf.at[at, pl.ds(i * RUN, RUN)], k1_ref, xs.at[i], h, c)
-        for when, act in events.items():
-            pl.when(g == when)(act)
         return carry
 
     lax.fori_loop(0, GROUPS // BATCH, chunk, 0)
 
     row_copies = [
-        send(st.at[pl.ds(own_start(7), 128), :], st.at[pl.ds(own_start(-1), 128), :], sems, 29, row_down),
-        send(st.at[pl.ds(own_start(0), 128), :], st.at[pl.ds(own_start(8), 128), :], sems, 30, row_up),
+        send(st.at[pl.ds(own_start(7), 128), :], st.at[pl.ds(own_start(-1), 128), :], sems, 56, row_down),
+        send(st.at[pl.ds(own_start(0), 128), :], st.at[pl.ds(own_start(8), 128), :], sems, 57, row_up),
     ]
     edge_copies = [
-        send(eout.at[0], ein.at[1], sems, 31, col_left),
-        send(eout.at[1], ein.at[0], sems, 32, col_right),
+        send(eout.at[0], ein.at[1], sems, 58, col_left),
+        send(eout.at[1], ein.at[0], sems, 59, col_right),
     ]
     corner_copies = [
-        send(cout.at[0], cin.at[1], sems, 33, row_up),
-        send(cout.at[1], cin.at[0], sems, 34, row_down),
+        send(cout.at[0], cin.at[1], sems, 60, row_up),
+        send(cout.at[1], cin.at[0], sems, 61, row_down),
     ]
+    pl.semaphore_wait(barrier, len(peers))
+    exchange.start()
     second_pass(3, k2_ref, eye_ref, m_ref, h, c, st)
     row_copies[0].start()
+    begin()
     second_pass(0, k2_ref, eye_ref, m_ref, h, c, st)
     row_copies[1].start()
-    forward(mid_second, last_first)()
     second_pass(1, k2_ref, eye_ref, m_ref, h, c, st)
+    forward(1)
     second_pass(2, k2_ref, eye_ref, m_ref, h, c, st)
     own_edges(st, et, eout)
     start(edge_copies)
+    forward(2)
     arrive(edge_copies)
     inner_edges(ein, st, et, cout)
     start(corner_copies)
-    gram_fields(st, f8, 2, 5, lambda i: i)
-    forward(last_first, last_second)()
+    forward(3)
+    gram_fields(st, f8, 2, 4, lambda i: i)
+    forward(4)
+    gram_fields(st, f8, 4, 5, lambda i: i)
     arrive(corner_copies)
     corner_edges(cin, st, et)
-    forward(last_second, final)()
     arrive(row_copies)
     gram_fields(st, f8, 0, 4, lambda i: i + 3 * (i // 2))
+    forward(5)
     weigh(f8, u, w)
     spread(w, wc, we)
-    arrive(final)
+    forward(6)
+    arrive(stages[6])
     entry_norms(d, inv)
     own_products(d, st, p)
     edge_products(d, st, et, p)
     edge_mix(p, we)
     best_scores(p, inv, wc, o_ref)
-    everything = [exchange] + y_first + y_second + mid_first + mid_second + last_first + last_second + final
-    for copy in everything + row_copies + edge_copies + corner_copies:
+    everything = [exchange] + row_copies + edge_copies + corner_copies
+    for stage in stages:
+        everything += stage
+    for copy in everything:
         copy.wait_send()
 
 
@@ -556,7 +539,7 @@
             pltpu.VMEM((BATCH, RUN * 8, 128), f32),
             pltpu.VMEM((4, GROUPS, RUN, 256), bf),
             pltpu.VMEM((4, GROUPS, GROUPS, 16, 256), f32),
-            pltpu.VMEM((4, 4, 64, DEPTH), bf),
+            pltpu.VMEM((4, 4, 4, 16, DEPTH), bf),
             pltpu.VMEM((8, DEPTH), f32),
             pltpu.VMEM((8, DEPTH), f32),
             pltpu.VMEM((HELD, DEPTH), bf),

time: 101 us -> 95.2 us (0.943)
  Pallas kernels: 99.8 us -> 93.5 us
    pallas_call x1, Pallas kernels: 99.8 us -> 93.5 us  [on_device(): pl.pallas_call(index_kernel, in_specs=[pl.BlockSpec(memory_space=pl.ANY)]...]
where the time goes in v3:
time: 95.2 us; the launch traced here: 94.9 us
  Pallas kernels  93.5 us (98%)
  local copies, waits for them, and re-layouts  1.38 us (1%)
    pallas_call x1, Pallas kernels, on_device(): pl.pallas_call(index_kernel, in_specs=[pl.BlockSpec(memory_space=pl.ANY)]...  93.5 us

profile of v3, /device:TPU:1, one launch (start us, length us, event | category | flops | bytes accessed | tf_op | source)
XLA Modules:
  0.0 94.9 jit_solution(14606510169134916103)
XLA Ops:
  0.0 93.5 %index.1 = f32[2,4,8,128]{3,2,1,0:T(8,128)} custom-call(bf16[3600,8,128]{2,1,0:T(8,128)(2,1)} %x_hbm.1, bf16[480,240]{1,0:T(8,128)(2,1)} %constant.8.clone.k1_ref, bf16[240,240]{1,0:T(8,128)(2,1)} %constant.9.clone.k2_ref, bf16[256,256]{1,0:T(8,128)(2,1)} %constant.10.clone.eye_ref, bf16[240,256]{1,0:T(8,128)(2,1)} %constant.11.clone.order_ref, ...), custom_call_target="tpu_custom_call" | custom-call | tf_op jit(solution)/shard_map/index/pallas_call | solution.py:532
  93.5 1.4 %copy.10 = f32[2,4,8,128]{3,2,1,0:T(8,128)} copy(f32[2,4,8,128]{3,2,1,0:T(8,128)} %index.1) | data formatting | bytes 65536

commit v4 on v2

--- a/solution.py
+++ b/solution.py
@@ -268,8 +268,7 @@
     lax.fori_loop(0, ROWS_DEV // 2, pair, 0)
 
 
-def edge_products(d, st, et, p):
-    pair_product(d, st, p, 0, ROWS_DEV + 1)
+def edge_products(d, et, p):
     edge = et[...].astype(jnp.bfloat16)
     edge = jnp.concatenate([edge, jnp.zeros((96, DEPTH), jnp.bfloat16)], axis=0)
     p[10] = lax.dot_general(d[...].reshape(1024, DEPTH), edge, NT, preferred_element_type=jnp.float32)
@@ -290,7 +289,7 @@
         p[10, at, :] = mix
         return carry
 
-    lax.fori_loop(0, 128, step, 0, unroll=8)
+    lax.fori_loop(0, 128, step, 0, unroll=16)
 
 
 def order(x, i, j):
@@ -391,9 +390,7 @@
     for peer in peers:
         pl.semaphore_signal(barrier, inc=1, device_id=peer, device_id_type=pl.DeviceIdType.MESH)
     prepare(dict_ref, order_ref, own)
-    pl.semaphore_wait(barrier, len(peers))
     exchange = send(own, sib, sems, 0, sibling)
-    exchange.start()
 
     base = pl.multiple_of(core * 1920, 128)
     half = pl.ds(base, 1920)
@@ -469,12 +466,6 @@
             start(following)
         return act
 
-    events = {
-        0: begin,
-        1: forward(y_first, y_second),
-        2: forward(y_second, mid_first),
-        4: forward(mid_first, mid_second),
-    }
     st[pl.ds(0, LEAD), :] = jnp.zeros((LEAD, DEPTH), jnp.bfloat16)
     tail = LANES - 10 * PITCH
     st[pl.ds(LEAD + 10 * PITCH, tail), :] = jnp.zeros((tail, DEPTH), jnp.bfloat16)
@@ -492,8 +483,6 @@
         fetch(g, at).wait()
         for i in range(BATCH):
             first_pass(g * BATCH + i, xbuf.at[at, pl.ds(i * RUN, RUN)], k1_ref, xs.at[i], h, c)
-        for when, act in events.items():
-            pl.when(g == when)(act)
         return carry
 
     lax.fori_loop(0, GROUPS // BATCH, chunk, 0)
@@ -510,31 +499,43 @@
         send(cout.at[0], cin.at[1], sems, 33, row_up),
         send(cout.at[1], cin.at[0], sems, 34, row_down),
     ]
+    def start_rows(turning):
+        pl.when((iy == 3) == turning)(row_copies[0].start)
+        pl.when((iy == 0) == turning)(row_copies[1].start)
+
+    pl.semaphore_wait(barrier, len(peers))
+    exchange.start()
     second_pass(3, k2_ref, eye_ref, m_ref, h, c, st)
-    row_copies[0].start()
+    begin()
     second_pass(0, k2_ref, eye_ref, m_ref, h, c, st)
-    row_copies[1].start()
-    forward(mid_second, last_first)()
     second_pass(1, k2_ref, eye_ref, m_ref, h, c, st)
+    forward(y_first, y_second)()
+    start_rows(False)
     second_pass(2, k2_ref, eye_ref, m_ref, h, c, st)
     own_edges(st, et, eout)
     start(edge_copies)
+    forward(y_second, mid_first)()
     arrive(edge_copies)
     inner_edges(ein, st, et, cout)
     start(corner_copies)
-    gram_fields(st, f8, 2, 5, lambda i: i)
+    forward(mid_first, mid_second)()
+    gram_fields(st, f8, 2, 4, lambda i: i)
+    forward(mid_second, last_first)()
+    gram_fields(st, f8, 4, 5, lambda i: i)
     forward(last_first, last_second)()
+    start_rows(True)
     arrive(corner_copies)
     corner_edges(cin, st, et)
     forward(last_second, final)()
+    arrive(final)
+    entry_norms(d, inv)
+    own_products(d, st, p)
+    edge_products(d, et, p)
     arrive(row_copies)
+    pair_product(d, st, p, 0, ROWS_DEV + 1)
     gram_fields(st, f8, 0, 4, lambda i: i + 3 * (i // 2))
     weigh(f8, u, w)
     spread(w, wc, we)
-    arrive(final)
-    entry_norms(d, inv)
-    own_products(d, st, p)
-    edge_products(d, st, et, p)
     edge_mix(p, we)
     best_scores(p, inv, wc, o_ref)
     everything = [exchange] + y_first + y_second + mid_first + mid_second + last_first + last_second + final

time: 101 us -> 95.8 us (0.949); the launches traced: 101 us -> 93.9 us
  Pallas kernels: 99.8 us -> 92.5 us
    pallas_call x1, Pallas kernels: 99.8 us -> 92.5 us  [on_device(): pl.pallas_call(index_kernel, in_specs=[pl.BlockSpec(memory_space=pl.ANY)]...]
where the time goes in v4:
time: 95.8 us; the launch traced here: 93.9 us
  Pallas kernels  92.5 us (97%)
  local copies, waits for them, and re-layouts  1.38 us (1%)
    pallas_call x1, Pallas kernels, on_device(): pl.pallas_call(index_kernel, in_specs=[pl.BlockSpec(memory_space=pl.ANY)]...  92.5 us

profile of v4, /device:TPU:1, one launch (start us, length us, event | category | flops | bytes accessed | tf_op | source)
XLA Modules:
  0.0 93.9 jit_solution(6544588717721225177)
XLA Ops:
  0.0 92.5 %index.1 = f32[2,4,8,128]{3,2,1,0:T(8,128)} custom-call(bf16[3600,8,128]{2,1,0:T(8,128)(2,1)} %x_hbm.1, bf16[480,240]{1,0:T(8,128)(2,1)} %constant.8.clone.k1_ref, bf16[240,240]{1,0:T(8,128)(2,1)} %constant.9.clone.k2_ref, bf16[256,256]{1,0:T(8,128)(2,1)} %constant.10.clone.eye_ref, bf16[240,256]{1,0:T(8,128)(2,1)} %constant.11.clone.order_ref, ...), custom_call_target="tpu_custom_call" | custom-call | tf_op jit(solution)/shard_map/index/pallas_call | solution.py:550
  92.5 1.4 %copy.10 = f32[2,4,8,128]{3,2,1,0:T(8,128)} copy(f32[2,4,8,128]{3,2,1,0:T(8,128)} %index.1) | data formatting | bytes 65536
